TPU v7x, 32 devices: a whole 2x2x4 slice. The times are simulated.
32 devices in a mesh: rows: 8 (over z, x), cols: 4 (over y, core).
Axes of the slice: x: 2, y: 2, z: 4, core: 2. Of those that a mesh axis runs over, the one named last changes fastest.
Arguments:
- panel_t: float32 [16, 2048], P(None, ('rows', 'cols')), may hold values from -6 to 6
- kinship: float32 [2048, 2048], P('rows', 'cols'), may hold values from -0.125 to 0.125
Outputs:
- kin_panel_t: float32 [16, 2048], P(None, ('rows', 'cols'))
- score: float32 [16, 16], replicated
All inputs are finite; a program needn't handle non-finite values.
Results may differ from a plain program's by a relative error of at most 0.00008.
Values sent between devices are 32-bit elements; how exact they have to be, the bound alone decides.
A program may use at most 64 MiB of HBM per device.

v0:
```python
import jax
import jax.numpy as jnp
from jax import lax
from jax.sharding import PartitionSpec as P


def contract(left, right):
    return lax.dot_general(
        left,
        right,
        (((1,), (1,)), ((), ())),
        precision=lax.Precision.HIGHEST,
        preferred_element_type=jnp.float32,
    )


def shards(panel_t, kinship):
    slab_rows, block_cols = kinship.shape
    row_index = lax.axis_index("rows")
    col_index = lax.axis_index("cols")
    gathered = lax.all_gather(panel_t, ("rows", "cols"), axis=1, tiled=True)
    slab_panel = lax.dynamic_slice_in_dim(gathered, row_index * slab_rows, slab_rows, 1)
    block_panel = lax.dynamic_slice_in_dim(gathered, col_index * block_cols, block_cols, 1)
    partial_value = contract(block_panel, kinship)
    scale = jnp.sqrt(jnp.float32(gathered.shape[1]))
    early_sum = lax.psum(contract(slab_panel, partial_value), ("rows", "cols"))
    kin_panel_t = lax.psum_scatter(partial_value, "cols", scatter_dimension=1, tiled=True)
    return (kin_panel_t, early_sum / scale)


def solution(mesh):
    placed = (P(None, ("rows", "cols")), P("rows", "cols"))
    return jax.shard_map(
        shards,
        mesh=mesh,
        in_specs=placed,
        out_specs=(P(None, ("rows", "cols")), P()),
        check_vma=False,
    )
```

profile of v0, /device:TPU:10, one launch (start us, length us, event | category | flops | bytes accessed | tf_op | source)
XLA Modules:
  0.0 99.6 jit_solution(12220211806638438616)
XLA Ops:
  7.2 0.0 copy-start
  7.2 0.0 reduce-scatter.4.cloned.1.call-start
  7.2 32.8 %all-gather = f32[32,64,16]{1,2,0:T(8,128)S(1)} all-gather(f32[1,64,16]{1,2,0:T(8,128)} %bitcast.11), channel_id=1, replica_groups=mesh['rows'=8,'cols'=4] {'rows','cols'}, dimensions={0}, use_global_device_ids=true | all-gather | bytes 135168 | tf_op jit(solution)/shard_map/all_gather | solution.py:21
  40.1 0.1 copy.5
  40.2 0.1 reshape.5
  40.3 0.0 copy-done
  40.3 0.5 fusion
  40.8 0.8 copy.6
  41.6 0.0 reduce-scatter.4.cloned.1.call-update
  41.6 0.1 fusion.2
  41.7 49.0 %psum.7 = f32[16,16]{1,0:T(8,128)S(1)} all-reduce(f32[16,16]{1,0:T(8,128)S(1)} %fusion.2), channel_id=1, replica_groups=mesh['rows'=8,'cols'=4] {'rows','cols'}, use_global_device_ids=true, to_apply=%region_1.0 | all-reduce | flops 256 | bytes 2048 | tf_op jit(solution)/shard_map/psum | solution.py:26
  90.7 0.6 broadcast_multiply_fusion
  91.3 0.0 reduce-scatter.4.cloned.1.call-done
  91.3 1.4 %copy.7 = f32[16,64]{1,0:T(8,128)} copy(f32[16,64]{0,1:T(8,128)} %bitcast.10) | data formatting | bytes 8192
Async XLA Ops:
  7.2 33.1 %copy-start = (f32[256,512]{1,0:T(8,128)S(1)}, f32[256,512]{1,0:T(8,128)}, u32[]{:S(2)}) copy-start(f32[256,512]{1,0:T(8,128)} %param.3) | copy-start | bytes 1572868
  7.2 84.1 %reduce-scatter.4.cloned.1.call-start = ((), (), s32[]{:S(2)}) async-start(), calls=%async_computation.1 | async-start | bytes 163840
Sparse Core Ops, SparseCore 0:
  41.7 25.6 reduce-scatter.3
where the time goes:
time: 99.9 us; the launch traced here: 99.6 us
  blocking collectives  81.8 us (82%)
  between operations  14.1 us (14%)
  local copies, waits for them, and re-layouts  2.39 us (2%)
    psum x1, blocking collectives, shards(): early_sum = lax.psum(contract(slab_panel, partial_value), ('rows', 'cols'))  49 us
    all_gather x1, blocking collectives, shards(): gathered = lax.all_gather(panel_t, ('rows', 'cols'), axis=1, tiled=True)  32.8 us
    unnamed x5, local copies, waits for them, and re-layouts  2.31 us
  transfers between devices with their start and end apart: 1, of which 0 were waited for; matrix products, arithmetic and copies ran while one was open for 1% of the time, Pallas kernels for 0%

commit v1 on v0

--- a/solution.py
+++ b/solution.py
@@ -23,7 +23,7 @@
     block_panel = lax.dynamic_slice_in_dim(gathered, col_index * block_cols, block_cols, 1)
     partial_value = contract(block_panel, kinship)
     scale = jnp.sqrt(jnp.float32(gathered.shape[1]))
-    early_sum = lax.psum(contract(slab_panel, partial_value), ("rows", "cols"))
+    early_sum = lax.psum(lax.psum(contract(slab_panel, partial_value), "cols"), "rows")
     kin_panel_t = lax.psum_scatter(partial_value, "cols", scatter_dimension=1, tiled=True)
     return (kin_panel_t, early_sum / scale)
 

time: 99.9 us -> 85.8 us (0.86)
  the two profiles are of different devices: /device:TPU:10 before, /device:TPU:0 now
where the time goes in v1:
time: 85.8 us; the launch traced here: 85.6 us
  blocking collectives  67.8 us (79%)
  between operations  14.1 us (16%)
  local copies, waits for them, and re-layouts  2.39 us (3%)
    all_gather x1, blocking collectives, shards(): gathered = lax.all_gather(panel_t, ('rows', 'cols'), axis=1, tiled=True)  44.3 us
    psum x1, blocking collectives, shards(): lax.psum(lax.psum(contract(slab_panel, partial_value), 'cols'), 'rows')  17.4 us
    psum x1, blocking collectives, shards(): lax.psum(contract(slab_panel, partial_value), 'cols')  6.11 us
    unnamed x5, local copies, waits for them, and re-layouts  2.31 us
  transfers between devices with their start and end apart: 1, of which 0 were waited for; matrix products, arithmetic and copies ran while one was open for 1% of the time, Pallas kernels for 0%

profile of v1, /device:TPU:0, one launch (start us, length us, event | category | flops | bytes accessed | tf_op | source)
XLA Modules:
  0.0 85.6 jit_solution(16316751144760683234)
XLA Ops:
  7.2 0.0 copy-start
  7.2 0.0 reduce-scatter.4.cloned.1.call-start
  7.2 44.3 %all-gather = f32[32,64,16]{1,2,0:T(8,128)S(1)} all-gather(f32[1,64,16]{1,2,0:T(8,128)} %bitcast.11), channel_id=1, replica_groups=mesh['rows'=8,'cols'=4] {'rows','cols'}, dimensions={0}, use_global_device_ids=true | all-gather | bytes 135168 | tf_op jit(solution)/shard_map/all_gather | solution.py:21
  51.6 0.1 copy.5
  51.7 0.1 reshape.5
  51.8 0.0 copy-done
  51.8 0.5 fusion
  52.3 0.8 copy.6
  53.1 0.0 reduce-scatter.4.cloned.1.call-update
  53.1 0.1 fusion.2
  53.2 6.1 %psum.14 = f32[16,16]{1,0:T(8,128)S(1)} all-reduce(f32[16,16]{1,0:T(8,128)S(1)} %fusion.2), channel_id=1, replica_groups=mesh['rows'=8,'cols'=4] {'cols'}, use_global_device_ids=true, to_apply=%region_1.0 | all-reduce | flops 256 | bytes 2048 | tf_op jit(solution)/shard_map/psum | solution.py:26
  59.3 17.4 %psum.15 = f32[16,16]{1,0:T(8,128)S(1)} all-reduce(f32[16,16]{1,0:T(8,128)S(1)} %psum.14), channel_id=1, replica_groups=mesh['rows'=8,'cols'=4] {'rows'}, use_global_device_ids=true, to_apply=%region_2.0 | all-reduce | flops 256 | bytes 2048 | tf_op jit(solution)/shard_map/psum | solution.py:26
  76.7 0.6 broadcast_multiply_fusion
  77.3 0.0 reduce-scatter.4.cloned.1.call-done
  77.3 1.4 %copy.7 = f32[16,64]{1,0:T(8,128)} copy(f32[16,64]{0,1:T(8,128)} %bitcast.10) | data formatting | bytes 8192
Async XLA Ops:
  7.2 44.6 %copy-start = (f32[256,512]{1,0:T(8,128)S(1)}, f32[256,512]{1,0:T(8,128)}, u32[]{:S(2)}) copy-start(f32[256,512]{1,0:T(8,128)} %param.3) | copy-start | bytes 1572868
  7.2 70.1 %reduce-scatter.4.cloned.1.call-start = ((), (), s32[]{:S(2)}) async-start(), calls=%async_computation.1 | async-start | bytes 163840
Sparse Core Ops, SparseCore 0:
  53.2 15.7 reduce-scatter.3
